TPU v7x, 32 devices: a whole 2x2x4 slice. The times are simulated.
32 devices in a mesh: loop: 8 (over y, x, core), tp: 4 (over z).
Axes of the slice: x: 2, y: 2, z: 4, core: 2. Of those that a mesh axis runs over, the one named last changes fastest.
Arguments:
- tokens: bfloat16 [2048, 4096], P('loop', 'tp'), may hold values from -6 to 6
- out_grad: bfloat16 [2048, 6144], P('loop', 'tp'), may hold values from -6 to 6
- qkv_weight: bfloat16 [3, 4096, 6144], P(None, 'loop', 'tp'), may hold values from -0.09375 to 0.09375
- dest_row: int32 [2048], P('loop'), may hold values from 0 to 383, as said below
- loop_modality: int32 [8], replicated, may hold values from 0 to 2, as said below
Outputs:
- projected: bfloat16 [2048, 6144], P('loop', 'tp')
- input_grad: bfloat16 [2048, 4096], P('loop', 'tp')
- weight_grad: bfloat16 [3, 4096, 6144], P(None, 'loop', 'tp')
Inputs may be any that keep to these rules, and one draw needn't show every extreme that they name: `dest_row`: within each aligned block of 256 tokens the values are distinct, so at most 48 tokens of one block name one loop; in every draw some loop is named by exactly 48 tokens of every block. `loop_modality`: A quarter of the loops hold 0, half hold 1, a quarter hold 2.
All inputs are finite; a program needn't handle non-finite values.
Results may differ from a plain program's by a relative error of at most 0.014.
Values may be sent and summed in bfloat16 or wider, within the bound.
No kernel may reach another device: no remote copies, remote signals or barrier semaphores. Data moves between devices by JAX's collectives and lax.ppermute only.
A program may use at most 128 MiB of HBM per device.

v0:
```python
import math

import jax
import jax.numpy as jnp
from jax import lax
from jax.sharding import PartitionSpec as P


def per_device(tokens, out_grad, qkv_weight, dest_row, loop_modality):
    loop_count = lax.axis_size("loop")
    row_count, feature_part = tokens.shape
    column_count = out_grad.shape[1]
    capacity = 3 * row_count // (2 * loop_count)
    slot_count = loop_count * capacity
    block_rows = qkv_weight.shape[1]
    grad_scale = 1.0 / math.sqrt(row_count * loop_count)
    token_send = jnp.zeros((slot_count, feature_part), jnp.bfloat16).at[dest_row].set(tokens)
    token_send = token_send.reshape(loop_count, capacity, feature_part)
    grad_send = jnp.zeros((slot_count, column_count), jnp.bfloat16).at[dest_row].set(out_grad)
    grad_send = grad_send.reshape(loop_count, capacity, column_count)
    loop_kinds = loop_modality[:, None, None]
    weight_send = jnp.where(
        loop_kinds == 0,
        qkv_weight[0][None],
        jnp.where(loop_kinds == 1, qkv_weight[1][None], qkv_weight[2][None]),
    )
    token_recv, grad_recv, weight_recv = (
        lax.all_to_all(token_send, "loop", split_axis=0, concat_axis=0, tiled=True),
        lax.all_to_all(grad_send, "loop", split_axis=0, concat_axis=0, tiled=True),
        lax.all_to_all(weight_send, "loop", split_axis=0, concat_axis=0, tiled=True),
    )
    token_rows = token_recv.reshape(slot_count, feature_part)
    grad_rows = grad_recv.reshape(slot_count, column_count)
    weight_full = weight_recv.reshape(loop_count * block_rows, column_count)
    projected = jnp.dot(
        lax.all_gather(token_rows, "tp", axis=1, tiled=True),
        weight_full,
        preferred_element_type=jnp.float32,
    )
    projected = projected.astype(jnp.bfloat16).reshape(loop_count, capacity, column_count)
    group_term = lax.dot_general(
        grad_rows, weight_full, (((1,), (1,)), ((), ())), preferred_element_type=jnp.float32
    )
    input_rows = lax.psum_scatter(
        group_term.astype(jnp.bfloat16), "tp", scatter_dimension=1, tiled=True
    )
    weight_part = (
        lax.dot_general(
            lax.all_gather(token_rows, "tp", axis=1, tiled=True),
            grad_rows,
            (((0,), (0,)), ((), ())),
            preferred_element_type=jnp.float32,
        )
        * grad_scale
    )
    received = lax.all_to_all(
        weight_part.reshape(loop_count, block_rows, column_count).astype(jnp.bfloat16),
        "loop",
        split_axis=0,
        concat_axis=0,
        tiled=True,
    ).astype(jnp.float32)
    merged = [
        jnp.sum(jnp.where((loop_modality == kind_index)[:, None, None], received, 0.0), axis=0)
        for kind_index in range(qkv_weight.shape[0])
    ]
    weight_grad = jnp.stack(merged).astype(jnp.bfloat16)
    input_send = input_rows.reshape(loop_count, capacity, feature_part)
    projected_back, input_back = (
        lax.all_to_all(projected, "loop", split_axis=0, concat_axis=0, tiled=True),
        lax.all_to_all(input_send, "loop", split_axis=0, concat_axis=0, tiled=True),
    )
    projected_rows = projected_back.reshape(slot_count, column_count)[dest_row]
    input_grad = input_back.reshape(slot_count, feature_part)[dest_row]
    return (projected_rows, input_grad, weight_grad)


def solution(mesh):
    placed = (P("loop", "tp"), P("loop", "tp"), P(None, "loop", "tp"), P("loop"), P())
    return jax.shard_map(
        per_device,
        mesh=mesh,
        in_specs=placed,
        out_specs=(P("loop", "tp"), P("loop", "tp"), P(None, "loop", "tp")),
        check_vma=False,
    )
```

profile of v0, /device:TPU:0, one launch (start us, length us, event | category | flops | bytes accessed | tf_op | source)
XLA Modules:
  0.0 384.7 jit_solution(10520052750600022554)
XLA Ops:
  7.2 0.7 compare_select_fusion
  7.8 3.1 scatter_custom_fusion
  10.9 5.2 %all-to-all-start = ((bf16[8,48,1024]{2,1,0:T(8,128)(2,1)}), bf16[8,48,1024]{2,1,0:T(8,128)(2,1)S(1)}, u32[]{:S(2)}, u32[]{:S(2)}) async-start(bf16[8,48,1024]{2,1,0:T(8,128)(2,1)} %bitcast), calls=%async_computation | async-start | bytes 1572864 | tf_op jit(solution)/shard_map/all_to_all | solution.py:28
  16.1 0.7 broadcast_compare_fusion
  16.8 2.7 slice_bitcast_fusion.2
  19.5 6.2 %select_select_fusion = bf16[8,512,1536]{2,1,0:T(8,128)(2,1)} fusion(pred[8]{0:T(512)(128)(4,1)S(1)} %get-tuple-element.11, pred[8]{0:T(512)(128)(4,1)S(1)} %get-tuple-element.10, bf16[512,1536]{1,0:T(8,128)(2,1)S(1)} %get-tuple-element.7, bf16[512,1536]{1,0:T(8,128)(2,1)S(1)} %get-tuple-element.8, bf16[512,1536]{1,0:T(8,128)(2,1)S(1)} %get-tuple-element.6), kind=kLoop, calls=%fused_computation.11 | loop fusion | flops 12582912 | bytes 17301520 | tf_op jit(solution)/shard_map/jit(_where)/select_n | solution.py:22
  25.6 3.1 all-to-all-done
  28.7 0.0 copy-start
  28.7 0.9 copy-done
  29.6 5.3 %all-to-all-start.1 = ((bf16[8,512,1536]{2,1,0:T(8,128)(2,1)}), bf16[8,512,1536]{2,1,0:T(8,128)(2,1)}, u32[]{:S(2)}, u32[]{:S(2)}) async-start(bf16[8,512,1536]{2,1,0:T(8,128)(2,1)} %select_select_fusion), calls=%async_computation.1 | async-start | bytes 25165824 | tf_op jit(solution)/shard_map/all_to_all | solution.py:30
  34.9 0.0 all-gather.2.cloned.1.call-start
  35.0 0.7 all-gather.2.cloned.1.call-update
  35.7 3.5 scatter_custom_fusion.1
  39.2 134.7 %all-to-all-done.1 = bf16[8,512,1536]{2,1,0:T(8,128)(2,1)} async-done(((bf16[8,512,1536]{2,1,0:T(8,128)(2,1)}), bf16[8,512,1536]{2,1,0:T(8,128)(2,1)}, u32[]{:S(2)}, u32[]{:S(2)}) %all-to-all-start.1) | async-done | bytes 12582944 | tf_op jit(solution)/shard_map/all_to_all | solution.py:30
  173.9 3.6 all-to-all-start.3
  177.5 0.0 all-gather.2.cloned.1.call-done
  177.5 11.1 %convolution_convert_fusion.1 = bf16[384,1536]{1,0:T(8,128)(2,1)} fusion(bf16[384,4096]{1,0:T(8,128)(2,1)} %all-gather.2.cloned.1.call-done, bf16[4096,1536]{1,0:T(8,128)(2,1)} %bitcast.5), kind=kOutput, calls=%fused_computation.14 | convolution fusion | flops 4832428032 | bytes 16908288 | tf_op jit(solution)/shard_map/dot_general | solution.py:35
  188.6 5.6 %all-to-all-done.3 = bf16[8,48,1536]{2,1,0:T(8,128)(2,1)S(1)} async-done(((bf16[8,48,1536]{2,1,0:T(8,128)(2,1)}), bf16[8,48,1536]{2,1,0:T(8,128)(2,1)S(1)}, u32[]{:S(2)}, u32[]{:S(2)}) %all-to-all-start.3) | async-done | bytes 1179680 | tf_op jit(solution)/shard_map/all_to_all | solution.py:29
  194.2 3.6 all-to-all-start.2
  197.8 11.6 %multiply_convert_fusion = bf16[4096,1536]{1,0:T(8,128)(2,1)} fusion(bf16[384,4096]{1,0:T(8,128)(2,1)} %all-gather.2.cloned.1.call-done, bf16[384,1536]{1,0:T(8,128)(2,1)S(1)} %bitcast.38), kind=kOutput, calls=%fused_computation.10 | convolution fusion | flops 4844421120 | bytes 16908288 | tf_op jit(solution)/shard_map/dot_general | solution.py:48
  209.4 5.1 %all-to-all-done.2 = bf16[8,48,1536]{2,1,0:T(8,128)(2,1)S(1)} async-done(((bf16[8,48,1536]{2,1,0:T(8,128)(2,1)}), bf16[8,48,1536]{2,1,0:T(8,128)(2,1)S(1)}, u32[]{:S(2)}, u32[]{:S(2)}) %all-to-all-start.2) | async-done | bytes 1179680 | tf_op jit(solution)/shard_map/all_to_all | solution.py:70
  214.5 5.4 %all-to-all-start.5 = ((bf16[8,512,1536]{2,1,0:T(8,128)(2,1)}), bf16[8,512,1536]{2,1,0:T(8,128)(2,1)}, u32[]{:S(2)}, u32[]{:S(2)}) async-start(bf16[8,512,1536]{2,1,0:T(8,128)(2,1)} %bitcast.33), calls=%async_computation.6 | async-start | bytes 25165824 | tf_op jit(solution)/shard_map/all_to_all | solution.py:56
  219.9 0.2 reduce-scatter.2.cloned.1.call-start
  220.1 18.1 %convolution_convert_fusion = bf16[384,4096]{1,0:T(8,128)(2,1)} fusion(bf16[384,1536]{1,0:T(8,128)(2,1)S(1)} %bitcast.39, bf16[4096,1536]{1,0:T(8,128)(2,1)} %bitcast.5), kind=kOutput, calls=%fused_computation.12 | convolution fusion | flops 4833411072 | bytes 16908288 | tf_op jit(solution)/shard_map/dot_general | solution.py:41
  238.2 0.0 reduce-scatter.2.cloned.1.call-update
  238.2 2.1 gather_fusion
  240.4 118.5 %all-to-all-done.5 = bf16[8,512,1536]{2,1,0:T(8,128)(2,1)} async-done(((bf16[8,512,1536]{2,1,0:T(8,128)(2,1)}), bf16[8,512,1536]{2,1,0:T(8,128)(2,1)}, u32[]{:S(2)}, u32[]{:S(2)}) %all-to-all-start.5) | async-done | bytes 12582944 | tf_op jit(solution)/shard_map/all_to_all | solution.py:56
  358.9 3.5 all-to-all-start.4
  362.4 11.0 %fusion = (bf16[512,1536]{1,0:T(8,128)(2,1)S(1)}, bf16[512,1536]{1,0:T(8,128)(2,1)S(1)}, bf16[512,1536]{1,0:T(8,128)(2,1)S(1)}) fusion(bf16[8,512,1536]{2,1,0:T(8,128)(2,1)} %all-to-all-done.5, pred[8]{0:T(512)(128)(4,1)S(1)} %get-tuple-element.10, pred[8]{0:T(512)(128)(4,1)S(1)} %get-tuple-element.11, pred[8]{0:T(512)(128)(4,1)S(1)} %get-tuple-element.9), kind=kLoop, calls=%fused_computation.7 | loop fusion | flops 41680896 | bytes 17301528 | tf_op jit(solution)/shard_map/reduce_sum | solution.py:64
  373.4 2.5 pad_maximum_fusion
  375.9 0.0 all-to-all-done.4
  375.9 2.0 gather_fusion.1
  (2 shorter events, 0.0 us)
Async XLA Ops:
  10.9 17.8 %all-to-all-start = ((bf16[8,48,1024]{2,1,0:T(8,128)(2,1)}), bf16[8,48,1024]{2,1,0:T(8,128)(2,1)S(1)}, u32[]{:S(2)}, u32[]{:S(2)}) async-start(bf16[8,48,1024]{2,1,0:T(8,128)(2,1)} %bitcast), calls=%async_computation | async-start | bytes 1572864 | tf_op jit(solution)/shard_map/all_to_all | solution.py:28
  28.7 0.9 copy-start
  29.6 144.3 %all-to-all-start.1 = ((bf16[8,512,1536]{2,1,0:T(8,128)(2,1)}), bf16[8,512,1536]{2,1,0:T(8,128)(2,1)}, u32[]{:S(2)}, u32[]{:S(2)}) async-start(bf16[8,512,1536]{2,1,0:T(8,128)(2,1)} %select_select_fusion), calls=%async_computation.1 | async-start | bytes 25165824 | tf_op jit(solution)/shard_map/all_to_all | solution.py:30
  34.9 142.6 %all-gather.2.cloned.1.call-start = ((), (), s32[]{:S(2)}) async-start(), calls=%async_computation.7 | async-start | bytes 3932160 | tf_op jit(solution)/shard_map/all_gather | solution.py:36
  173.9 20.3 %all-to-all-start.3 = ((bf16[8,48,1536]{2,1,0:T(8,128)(2,1)}), bf16[8,48,1536]{2,1,0:T(8,128)(2,1)S(1)}, u32[]{:S(2)}, u32[]{:S(2)}) async-start(bf16[8,48,1536]{2,1,0:T(8,128)(2,1)} %bitcast.8), calls=%async_computation.3 | async-start | bytes 2359296 | tf_op jit(solution)/shard_map/all_to_all | solution.py:29
  194.2 20.3 %all-to-all-start.2 = ((bf16[8,48,1536]{2,1,0:T(8,128)(2,1)}), bf16[8,48,1536]{2,1,0:T(8,128)(2,1)S(1)}, u32[]{:S(2)}, u32[]{:S(2)}) async-start(bf16[8,48,1536]{2,1,0:T(8,128)(2,1)} %bitcast.6), calls=%async_computation.2 | async-start | bytes 2359296 | tf_op jit(solution)/shard_map/all_to_all | solution.py:70
  214.5 144.4 %all-to-all-start.5 = ((bf16[8,512,1536]{2,1,0:T(8,128)(2,1)}), bf16[8,512,1536]{2,1,0:T(8,128)(2,1)}, u32[]{:S(2)}, u32[]{:S(2)}) async-start(bf16[8,512,1536]{2,1,0:T(8,128)(2,1)} %bitcast.33), calls=%async_computation.6 | async-start | bytes 25165824 | tf_op jit(solution)/shard_map/all_to_all | solution.py:56
  219.9 139.0 %reduce-scatter.2.cloned.1.call-start = ((), (), s32[]{:S(2)}) async-start(), calls=%async_computation.8 | async-start | bytes 3932160 | tf_op jit(solution)/shard_map/reduce_scatter | solution.py:44
  358.9 17.0 %all-to-all-start.4 = ((bf16[8,48,1024]{2,1,0:T(8,128)(2,1)}), bf16[8,48,1024]{2,1,0:T(8,128)(2,1)S(1)}, u32[]{:S(2)}, u32[]{:S(2)}) async-start(bf16[8,48,1024]{2,1,0:T(8,128)(2,1)} %bitcast.40), calls=%async_computation.5 | async-start | bytes 1572864 | tf_op jit(solution)/shard_map/all_to_all | solution.py:71
Sparse Core Ops, SparseCore 0:
  37.9 65.0 all-gather.1
  238.3 61.7 reduce-scatter.1
where the time goes:
time: 385 us
  waiting for transfers between devices  268 us (70%)
  matrix products  40.8 us (11%)
  starting transfers between devices  26.9 us (7%)
  other arithmetic  20.9 us (5%)
  local copies, waits for them, and re-layouts  14.3 us (4%)
  between operations  14.1 us (4%)
    all_to_all x1, waiting for transfers between devices, per_device(): lax.all_to_all(weight_send, 'loop', split_axis=0, concat_axis=0, tiled=True)  135 us
    all_to_all x1, waiting for transfers between devices, per_device(): lax.all_to_all(weight_part.reshape(loop_count, block_rows, column_count)....  119 us
    dot_general x1, matrix products, per_device(): lax.dot_general(grad_rows, weight_full, (((1,), (1,)), ((), ())), preferr...  18.1 us
    dot_general x1, matrix products, per_device(): lax.dot_general(lax.all_gather(token_rows, 'tp', axis=1, tiled=True), gra...  11.6 us
    dot_general x1, matrix products, per_device(): jnp.dot(lax.all_gather(token_rows, 'tp', axis=1, tiled=True), weight_full...  11.1 us
    reduce_sum x1, other arithmetic, per_device(): jnp.sum(jnp.where((loop_modality == kind_index)[:, None, None], received,...  11 us
  transfers between devices with their start and end apart: 8, of which 5 were waited for; matrix products, arithmetic and copies ran while one was open for 18% of the time, Pallas kernels for 0%

commit v1 on v0

v1 whole, which is shorter than its diff:
```python
import math

import jax
import jax.numpy as jnp
from jax import lax
from jax.sharding import PartitionSpec as P


def per_device(tokens, out_grad, qkv_weight, dest_row, loop_modality):
    loop_count = lax.axis_size("loop")
    row_count, feature_part = tokens.shape
    kinds, block_rows, column_count = qkv_weight.shape
    capacity = 3 * row_count // (2 * loop_count)
    grad_scale = 1.0 / math.sqrt(row_count * loop_count)
    own_kind = loop_modality[dest_row // capacity]
    kind_of = lax.all_gather(own_kind, "loop", axis=0, tiled=True)
    grads = lax.all_gather(out_grad, "loop", axis=0, tiled=True)
    features = lax.all_gather(tokens, "tp", axis=1, tiled=True)
    rows = lax.all_to_all(features, "loop", split_axis=1, concat_axis=0, tiled=True)
    masks = [(kind_of == kind)[:, None] for kind in range(kinds)]
    term = sum(
        lax.dot_general(
            jnp.where(masks[kind], grads, 0), qkv_weight[kind], (((1,), (1,)), ((), ())),
            preferred_element_type=jnp.float32,
        )
        for kind in range(kinds)
    ).astype(jnp.bfloat16)
    term = lax.all_to_all(term, "loop", split_axis=0, concat_axis=1, tiled=True)
    input_grad = lax.psum_scatter(term, "tp", scatter_dimension=1, tiled=True)
    partial = sum(
        jnp.dot(jnp.where(masks[kind], rows, 0), qkv_weight[kind], preferred_element_type=jnp.float32)
        for kind in range(kinds)
    ).astype(jnp.bfloat16)
    projected = lax.psum_scatter(partial, "loop", scatter_dimension=0, tiled=True)
    weight_grad = jnp.stack([
        (
            lax.dot_general(
                jnp.where(masks[kind], rows, 0), grads, (((0,), (0,)), ((), ())),
                preferred_element_type=jnp.float32,
            )
            * grad_scale
        ).astype(jnp.bfloat16)
        for kind in range(kinds)
    ])
    return projected, input_grad, weight_grad


def solution(mesh):
    placed = (P("loop", "tp"), P("loop", "tp"), P(None, "loop", "tp"), P("loop"), P())
    return jax.shard_map(
        per_device,
        mesh=mesh,
        in_specs=placed,
        out_specs=(P("loop", "tp"), P("loop", "tp"), P(None, "loop", "tp")),
        check_vma=False,
    )
```

time: 385 us -> 279 us (0.72)
  waiting for transfers between devices: 268 us -> 88.1 us
  blocking collectives: 0 us -> 78.1 us
  starting transfers between devices: 26.9 us -> 3.99 us
  matrix products: 40.8 us -> 61.7 us
  other arithmetic: 20.9 us -> 14.1 us
  local copies, waits for them, and re-layouts: 14.3 us -> 18.6 us
    all_to_all x6 -> x1, waiting for transfers between devices: 267 us -> 0.01 us  [per_device(): lax.all_to_all(features, 'loop', split_axis=1, concat_axis=0, tiled=True)]
    all_gather x1 -> x2, waiting for transfers between devices: 0.02 us -> 48.5 us  [the longest x1 48.5 us: per_device(): features = lax.all_gather(tokens, 'tp', axis=1, tiled=True)]
    all_to_all x0 -> x1, blocking collectives: none -> 45.9 us  [per_device(): term = lax.all_to_all(term, 'loop', split_axis=0, concat_axis=1, tiled=True)]
    reduce_scatter x1 -> x2, waiting for transfers between devices: 0.01 us -> 38.8 us  [the longest x1 38.8 us: per_device(): input_grad = lax.psum_scatter(term, 'tp', scatter_dimension=1, tiled=True)]
    all_gather x0 -> x1, blocking collectives: none -> 32.2 us  [per_device(): kind_of = lax.all_gather(own_kind, 'loop', axis=0, tiled=True)]
    all_to_all x6 -> x1, starting transfers between devices: 26.6 us -> 3.65 us  [per_device(): lax.all_to_all(features, 'loop', split_axis=1, concat_axis=0, tiled=True)]
    dot_general x3 -> x9, matrix products: 40.8 us -> 61.7 us  [the longest x3 31.3 us: per_device(): jnp.dot(jnp.where(masks[kind], rows, 0), qkv_weight[kind], preferred_elem...]
    select_n x0 -> x3, local copies, waits for them, and re-layouts: none -> 11.8 us  [per_device(): jnp.where(masks[kind], rows, 0)]
  transfers between devices with their start and end apart: 8 -> 5, of which waited for: 5 -> 2; matrix products, arithmetic and copies ran while one was open for 18% -> 33% of each run, Pallas kernels for 0% -> 0%
where the time goes in v1:
time: 279 us
  waiting for transfers between devices  88.1 us (32%)
  blocking collectives  78.1 us (28%)
  matrix products  61.7 us (22%)
  local copies, waits for them, and re-layouts  18.6 us (7%)
  other arithmetic  14.1 us (5%)
  between operations  13.9 us (5%)
  starting transfers between devices  3.99 us (1%)
    all_gather x1, waiting for transfers between devices, per_device(): features = lax.all_gather(tokens, 'tp', axis=1, tiled=True)  48.5 us
    all_to_all x1, blocking collectives, per_device(): term = lax.all_to_all(term, 'loop', split_axis=0, concat_axis=1, tiled=True)  45.9 us
    reduce_scatter x1, waiting for transfers between devices, per_device(): input_grad = lax.psum_scatter(term, 'tp', scatter_dimension=1, tiled=True)  38.8 us
    all_gather x1, blocking collectives, per_device(): kind_of = lax.all_gather(own_kind, 'loop', axis=0, tiled=True)  32.2 us
    dot_general x3, matrix products, per_device(): jnp.dot(jnp.where(masks[kind], rows, 0), qkv_weight[kind], preferred_elem...  31.3 us
    dot_general x3, matrix products, per_device(): lax.dot_general(jnp.where(masks[kind], grads, 0), qkv_weight[kind], (((1,...  16.7 us
    dot_general x3, matrix products, per_device(): lax.dot_general(jnp.where(masks[kind], rows, 0), grads, (((0,), (0,)), ((...  13.6 us
    select_n x3, local copies, waits for them, and re-layouts, per_device(): jnp.where(masks[kind], rows, 0)  11.8 us
  transfers between devices with their start and end apart: 5, of which 2 were waited for; matrix products, arithmetic and copies ran while one was open for 33% of the time, Pallas kernels for 0%

profile of v1, /device:TPU:0, one launch (start us, length us, event | category | flops | bytes accessed | tf_op | source)
XLA Modules:
  0.0 278.5 jit_solution(15667492491029857206)
XLA Ops:
  7.2 0.0 all-gather.5.cloned.1.call-start
  7.2 2.0 copy.17
  9.3 0.0 all-gather.5.cloned.1.call-update
  9.3 0.0 all-gather.7.cloned.1.call-start
  9.3 0.7 all-gather.7.cloned.1.call-update
  10.0 48.5 %all-gather.5.cloned.1.call-done = bf16[256,4096]{0,1:T(8,128)(2,1)} async-done(((bf16[256,1024]{0,1:T(8,128)(2,1)}), bf16[256,4096]{0,1:T(8,128)(2,1)}) %all-gather.5.cloned.1.call-update) | async-done | bytes 2097168 | tf_op jit(solution)/shard_map/all_gather | solution.py:18
  58.5 3.7 %all-to-all-start = ((bf16[256,8,512]{0,2,1:T(8,128)(2,1)}), bf16[256,8,512]{0,2,1:T(8,128)(2,1)S(1)}, u32[]{:S(2)}, u32[]{:S(2)}) async-start(bf16[256,8,512]{0,2,1:T(8,128)(2,1)} %bitcast.68), calls=%async_computation | async-start | bytes 4194304 | tf_op jit(solution)/shard_map/all_to_all | solution.py:19
  62.2 0.0 reduce-scatter.3.cloned.1.call-start
  62.3 0.7 fusion.37
  63.0 5.2 %compare_select_fusion.1 = s32[256]{0:T(256)S(1)} fusion(s32[256]{0:T(256)S(1)} %copy-done.3, s32[]{:T(128)} %bitcast, s32[]{:T(128)} %bitcast.1, s32[]{:T(128)} %bitcast.2, s32[]{:T(128)} %bitcast.3, s32[]{:T(128)} %bitcast.4, s32[]{:T(128)} %bitcast.5, s32[]{:T(128)} %bitcast.6, s32[]{:T(128)} %bitcast.7), kind=kLoop, calls=%fused_computation.48 | loop fusion | flops 6400 | bytes 2080 | tf_op jit(solution)/shard_map/gather | solution.py:15
  68.1 32.2 %all-gather.1 = s32[8,1,256]{2,1,0:T(1,128)S(1)} all-gather(s32[1,1,256]{2,1,0:T(1,128)S(1)} %bitcast.75), channel_id=2, replica_groups=mesh['loop'=8,'tp'=4] {'loop'}, dimensions={0}, use_global_device_ids=true | all-gather | bytes 9216 | tf_op jit(solution)/shard_map/all_gather | solution.py:16
  100.3 2.8 %broadcast_select_fusion = (bf16[8,256,512]{1,2,0:T(8,128)(2,1)}, bf16[8,256,512]{1,2,0:T(8,128)(2,1)}, bf16[8,256,512]{1,2,0:T(8,128)(2,1)}) fusion(pred[8,256]{1,0:T(8,128)(4,1)S(1)} %bitcast.72, bf16[256,8,512]{0,2,1:T(8,128)(2,1)S(1)} %all-to-all-done, pred[8,256]{1,0:T(8,128)(4,1)S(1)} %bitcast.74, pred[8,256]{1,0:T(8,128)(4,1)S(1)} %bitcast.73), kind=kLoop, calls=%fused_computation.27 | loop fusion | flops 3145728 | bytes 8394752 | tf_op jit(solution)/shard_map/jit(_where)/select_n | solution.py:31
  103.2 3.9 %copy.20 = bf16[8,256,512]{2,1,0:T(8,128)(2,1)} copy(bf16[8,256,512]{1,2,0:T(8,128)(2,1)} %get-tuple-element.8) | data formatting | bytes 4194304 | tf_op jit(solution)/shard_map/jit(_where)/select_n | solution.py:31
  107.1 4.0 %copy.18 = bf16[8,256,512]{2,1,0:T(8,128)(2,1)} copy(bf16[8,256,512]{1,2,0:T(8,128)(2,1)} %get-tuple-element.7) | data formatting | bytes 4194304 | tf_op jit(solution)/shard_map/jit(_where)/select_n | solution.py:31
  111.1 3.9 %copy.22 = bf16[8,256,512]{2,1,0:T(8,128)(2,1)} copy(bf16[8,256,512]{1,2,0:T(8,128)(2,1)} %get-tuple-element.6) | data formatting | bytes 4194304 | tf_op jit(solution)/shard_map/jit(_where)/select_n | solution.py:31
  115.0 10.2 %fusion.23 = f32[2048,1536]{1,0:T(8,128)} fusion(bf16[2048,512]{1,0:T(8,128)(2,1)} %bitcast.69, bf16[3,512,1536]{2,1,0:T(8,128)(2,1)} %param.7), kind=kOutput, calls=%fused_computation.33 | convolution fusion | flops 3221225472 | bytes 16252928 | tf_op jit(solution)/shard_map/dot_general | solution.py:31
  125.2 7.8 %fusion.26 = f32[2048,1536]{1,0:T(8,128)} fusion(bf16[2048,512]{1,0:T(8,128)(2,1)S(1)} %bitcast.70, bf16[3,512,1536]{2,1,0:T(8,128)(2,1)} %param.7), kind=kOutput, calls=%fused_computation.36 | convolution fusion | flops 3221225472 | bytes 16252928 | tf_op jit(solution)/shard_map/dot_general | solution.py:31
  133.0 13.3 %add_convert_fusion = bf16[2048,1536]{1,0:T(8,128)(2,1)} fusion(f32[2048,1536]{1,0:T(8,128)} %fusion.26, f32[2048,1536]{1,0:T(8,128)} %fusion.23, bf16[2048,512]{1,0:T(8,128)(2,1)S(1)} %bitcast.65, bf16[3,512,1536]{2,1,0:T(8,128)(2,1)} %param.7), kind=kOutput, calls=%fused_computation | convolution fusion | flops 3230662656 | bytes 35127296 | tf_op jit(solution)/shard_map/dot_general | solution.py:31
  146.4 0.2 reduce-scatter.5.cloned.1.call-start
  146.6 0.0 all-gather.7.cloned.1.call-done
  146.7 6.3 %fusion = f32[2048,512]{1,0:T(8,128)S(1)} fusion(bf16[2048,1536]{1,0:T(8,128)(2,1)} %all-gather.7.cloned.1.call-done, pred[2048]{0:T(1024)(128)(4,1)S(1)} %reshape.57, bf16[3,512,1536]{2,1,0:T(8,128)(2,1)} %param.7), kind=kOutput, calls=%fused_computation.1 | convolution fusion | flops 3224371200 | bytes 12060672 | tf_op jit(solution)/shard_map/dot_general | solution.py:22
  153.0 5.2 %fusion.2 = f32[2048,512]{1,0:T(8,128)S(1)} fusion(bf16[2048,1536]{1,0:T(8,128)(2,1)S(1)} %copy-done.4, pred[2048]{0:T(1024)(128)(4,1)S(1)} %reshape.55, bf16[3,512,1536]{2,1,0:T(8,128)(2,1)} %param.7), kind=kOutput, calls=%fused_computation.3 | convolution fusion | flops 3224371200 | bytes 12060672 | tf_op jit(solution)/shard_map/dot_general | solution.py:22
  158.2 5.2 %add_convert_fusion.1 = bf16[2048,512]{1,0:T(8,128)(2,1)S(1)} fusion(f32[2048,512]{1,0:T(8,128)S(1)} %fusion, f32[2048,512]{1,0:T(8,128)S(1)} %fusion.2, bf16[2048,1536]{1,0:T(8,128)(2,1)S(1)} %copy-done.4, pred[2048]{0:T(1024)(128)(4,1)S(1)} %reshape.53, bf16[3,512,1536]{2,1,0:T(8,128)(2,1)} %param.7), kind=kOutput, calls=%fused_computation.11 | convolution fusion | flops 3227516928 | bytes 18352128 | tf_op jit(solution)/shard_map/dot_general | solution.py:22
  163.4 45.9 %all_to_all.38 = bf16[8,256,512]{2,1,0:T(8,128)(2,1)S(1)} all-to-all(bf16[8,256,512]{2,1,0:T(8,128)(2,1)S(1)} %bitcast.71), channel_id=1, replica_groups=mesh['loop'=8,'tp'=4] {'loop'}, dimensions={0} | all-to-all | bytes 4194304 | tf_op jit(solution)/shard_map/all_to_all | solution.py:28
  209.3 1.6 copy.25
  210.9 2.4 copy.24
  213.3 3.7 %bitcast_select_fusion.2 = (bf16[2048,512]{1,0:T(8,128)(2,1)S(1)}, bf16[2048,512]{1,0:T(8,128)(2,1)S(1)}, bf16[2048,512]{1,0:T(8,128)(2,1)S(1)}) fusion(bf16[8,256,512]{2,1,0:T(8,128)(2,1)} %copy.24, pred[2048]{0:T(1024)(128)(4,1)S(1)} %reshape.53, pred[2048]{0:T(1024)(128)(4,1)S(1)} %reshape.55, pred[2048]{0:T(1024)(128)(4,1)S(1)} %reshape.57), kind=kLoop, calls=%fused_computation.26 | loop fusion | flops 3145728 | bytes 8394752 | tf_op jit(solution)/shard_map/jit(_where)/select_n | solution.py:31
  217.0 6.5 %fusion.15 = bf16[1,512,1536]{2,1,0:T(8,128)(2,1)S(1)} fusion(bf16[2048,512]{1,0:T(8,128)(2,1)S(1)} %get-tuple-element.5, bf16[2048,1536]{1,0:T(8,128)(2,1)} %all-gather.7.cloned.1.call-done), kind=kOutput, calls=%fused_computation.21 | convolution fusion | flops 3222798336 | bytes 9961472 | tf_op jit(solution)/shard_map/dot_general | solution.py:37
  223.5 3.6 %fusion.16 = bf16[1,512,1536]{2,1,0:T(8,128)(2,1)S(1)} fusion(bf16[2048,512]{1,0:T(8,128)(2,1)S(1)} %get-tuple-element.4, bf16[2048,1536]{1,0:T(8,128)(2,1)S(1)} %bitcast.77), kind=kOutput, calls=%fused_computation.22 | convolution fusion | flops 3222798336 | bytes 9961472 | tf_op jit(solution)/shard_map/dot_general | solution.py:37
  227.1 3.6 %fusion.17 = bf16[1,512,1536]{2,1,0:T(8,128)(2,1)S(1)} fusion(bf16[2048,512]{1,0:T(8,128)(2,1)S(1)} %get-tuple-element.3, bf16[2048,1536]{1,0:T(8,128)(2,1)S(1)} %bitcast.77), kind=kOutput, calls=%fused_computation.23 | convolution fusion | flops 3222798336 | bytes 9961472 | tf_op jit(solution)/shard_map/dot_general | solution.py:37
  230.7 2.5 pad_maximum_fusion
  233.2 38.8 %reduce-scatter.5.cloned.1.call-done = bf16[256,1024]{1,0:T(8,128)(2,1)} async-done(((bf16[256,4096]{1,0:T(8,128)(2,1)}), bf16[256,1024]{1,0:T(8,128)(2,1)}) %reduce-scatter.5.cloned.1.call-update) | async-done | bytes 524304 | tf_op jit(solution)/shard_map/reduce_scatter | solution.py:29
  (23 shorter events, 0.1 us)
Async XLA Ops:
  7.2 55.1 %copy-start.2 = (s32[8]{0:T(128)S(1)}, s32[8]{0:T(128)}, u32[]{:S(2)}) copy-start(s32[8]{0:T(128)} %param.9) | copy-start | bytes 100
  7.2 55.8 %copy-start.3 = (s32[256]{0:T(256)S(1)}, s32[256]{0:T(256)}, u32[]{:S(2)}) copy-start(s32[256]{0:T(256)} %param.8) | copy-start | bytes 3076
  7.2 51.4 %all-gather.5.cloned.1.call-start = ((), (), s32[]{:S(2)}) async-start(), calls=%async_computation.4 | async-start | bytes 2621440 | tf_op jit(solution)/shard_map/all_gather | solution.py:18
  9.3 137.4 %all-gather.7.cloned.1.call-start = ((), (), s32[]{:S(2)}) async-start(), calls=%async_computation.6 | async-start | bytes 7077888 | tf_op jit(solution)/shard_map/all_gather | solution.py:17
  58.5 41.8 %all-to-all-start = ((bf16[256,8,512]{0,2,1:T(8,128)(2,1)}), bf16[256,8,512]{0,2,1:T(8,128)(2,1)S(1)}, u32[]{:S(2)}, u32[]{:S(2)}) async-start(bf16[256,8,512]{0,2,1:T(8,128)(2,1)} %bitcast.68), calls=%async_computation | async-start | bytes 4194304 | tf_op jit(solution)/shard_map/all_to_all | solution.py:19
  62.2 171.0 %reduce-scatter.3.cloned.1.call-start = ((), (), s32[]{:S(2)}) async-start(), calls=%async_computation.5 | async-start | bytes 7077888 | tf_op jit(solution)/shard_map/reduce_scatter | solution.py:34
  115.0 10.2 %copy-start.1 = (bf16[8,256,512]{2,1,0:T(8,128)(2,1)S(1)}, bf16[8,256,512]{2,1,0:T(8,128)(2,1)}, u32[]{:S(2)}) copy-start(bf16[8,256,512]{2,1,0:T(8,128)(2,1)} %copy.18) | copy-start | bytes 6291460
  125.2 7.9 %copy-start = (bf16[8,256,512]{2,1,0:T(8,128)(2,1)S(1)}, bf16[8,256,512]{2,1,0:T(8,128)(2,1)}, u32[]{:S(2)}) copy-start(bf16[8,256,512]{2,1,0:T(8,128)(2,1)} %copy.22) | copy-start | bytes 6291460
  146.4 125.6 %reduce-scatter.5.cloned.1.call-start = ((), (), s32[]{:S(2)}) async-start(), calls=%async_computation.7 | async-start | bytes 2621440 | tf_op jit(solution)/shard_map/reduce_scatter | solution.py:29
  146.7 6.3 %copy-start.4 = (bf16[2048,1536]{1,0:T(8,128)(2,1)S(1)}, bf16[2048,1536]{1,0:T(8,128)(2,1)}, u32[]{:S(2)}) copy-start(bf16[2048,1536]{1,0:T(8,128)(2,1)} %all-gather.7.cloned.1.call-done) | copy-start | bytes 18874372
  213.3 10.2 %slice-start = ((s8[6291456]{0:T(1024)(128)(4,1)}), s8[4194304]{0:T(1024)(128)(4,1)S(1)}, s32[]{:S(2)}) async-start(s8[6291456]{0:T(1024)(128)(4,1)} %bitcast.76), calls=%async_computation.8 | async-start | bytes 8388608
  217.0 6.5 %slice-start.1 = ((s8[6291456]{0:T(1024)(128)(4,1)}), s8[2097152]{0:T(1024)(128)(4,1)S(1)}, s32[]{:S(2)}) async-start(s8[6291456]{0:T(1024)(128)(4,1)} %bitcast.76), calls=%async_computation.9 | async-start | bytes 4194304
Sparse Core Ops, SparseCore 0:
  10.1 48.3 all-gather.4
  60.4 58.3 all-gather.6
  146.5 79.0 reduce-scatter.2
  228.3 43.6 reduce-scatter.4
